TPU v7x, 512 devices: a whole 4x8x8 slice. The times are simulated.
512 devices in a mesh: seq: 32 (over z_lo, y, core), head: 16 (over x, z_hi).
Axes of the slice: x: 4, y: 8, z: 8 (z_hi: 4, z_lo: 2; z = z_hi * 2 + z_lo), core: 2. Of those that a mesh axis runs over, the one named last changes fastest.
Arguments:
- q_nope: bfloat16 [3072, 16384], P('seq', 'head'), may hold values from -6 to 6
- q_rope: bfloat16 [3072, 8192], P('seq', 'head'), may hold values from -48 to 48
- w_uk: bfloat16 [128, 128, 512], P('head'), may hold values from -0.5 to 0.5
- w_uv: bfloat16 [128, 512, 128], P('head'), may hold values from -0.25 to 0.25
- w_value: float32 [16384], P('head'), may hold values from -0.1875 to 0.1875
- kv_cache: bfloat16 [4096, 576], P('seq'), may hold values from -8 to 8
- cutoffs: int32 [3072], P('seq'), may hold values from 1 to 4096, as said below
Outputs:
- attn: bfloat16 [3072, 16384], P('seq', 'head')
- value: float32 [3072], P('seq')
Inputs may be any that keep to these rules, and one draw needn't show every extreme that they name: `cutoffs`: every row sees at least the first event; some row sees the whole history and some row only the first event.
All inputs are finite; a program needn't handle non-finite values.
Results may differ from a plain program's by a relative error of at most 0.014.
Values may be sent and summed in bfloat16 or wider, within the bound.
A program may use at most 64 MiB of HBM per device.

v0:
```python
import jax
import jax.numpy as jnp
from jax import lax
from jax.sharding import PartitionSpec as P

softmax_scale = (128.0 + 64.0) ** (-0.5)


def on_device(q_nope, q_rope, w_uk, w_uv, w_value, kv_cache, cutoffs):
    rows = q_nope.shape[0]
    heads = w_uk.shape[0]
    latent = w_uk.shape[2]
    nope_rows = q_nope.reshape(rows, heads, w_uk.shape[1])
    q_lat = jnp.einsum("rhn,hnc->rhc", nope_rows, w_uk, preferred_element_type=jnp.float32).astype(
        jnp.bfloat16
    )
    q_all = jnp.concatenate([q_lat, q_rope.reshape(rows, heads, -1)], axis=2)
    piece = lax.all_gather(kv_cache, "seq", axis=0, tiled=True)
    running = jnp.full((rows, heads), -1e30, jnp.float32)
    count = piece.shape[0]
    score = (
        jnp.einsum("rhc,ec->rhe", q_all, piece, preferred_element_type=jnp.float32) * softmax_scale
    )
    index = jnp.arange(count, dtype=jnp.int32)
    keep = index[None, None, :] < cutoffs[:, None, None]
    score = jnp.where(keep, score, -jnp.inf)
    newest = jnp.maximum(running, jnp.max(score, axis=2))
    weight = jnp.exp(score - newest[:, :, None])
    total = jnp.sum(weight, axis=2)
    update = jnp.einsum(
        "rhe,ec->rhc",
        weight.astype(jnp.bfloat16),
        piece[:, :latent],
        preferred_element_type=jnp.float32,
    )
    accum = update
    running, total, accum = (newest, total, accum)
    o_lat = (accum / total[:, :, None]).astype(jnp.bfloat16)
    attn = jnp.einsum("rhc,hcv->rhv", o_lat, w_uv, preferred_element_type=jnp.float32).astype(
        jnp.bfloat16
    )
    attn = attn.reshape(rows, -1)
    partial_score = jnp.sum(attn.astype(jnp.float32) * w_value[None, :], axis=1)
    value = lax.psum(partial_score, "head")
    return (attn, value)


def solution(mesh):
    placed = (
        P("seq", "head"),
        P("seq", "head"),
        P("head", None, None),
        P("head", None, None),
        P("head"),
        P("seq", None),
        P("seq"),
    )
    return jax.shard_map(
        on_device,
        mesh=mesh,
        in_specs=placed,
        out_specs=(P("seq", "head"), P("seq")),
        check_vma=False,
    )
```

profile of v0, /device:TPU:16, one launch (start us, length us, event | category | flops | bytes accessed | tf_op | source)
XLA Modules:
  0.0 163.2 jit_solution(10106467120380042580)
XLA Ops:
  7.2 0.0 copy-start
  7.2 0.0 all-gather.2.cloned.1.call-start
  7.2 0.7 all-gather.2.cloned.1.call-update
  7.9 1.0 copy.13
  8.9 0.2 copy.14
  9.1 0.0 copy-done
  9.1 1.3 fusion.11
  10.4 0.1 pad_maximum_fusion
  10.5 1.0 iota_compare_fusion
  11.4 79.9 %all-gather.2.cloned.1.call-done = bf16[4096,576]{0,1:T(8,128)(2,1)} async-done(((bf16[128,576]{0,1:T(8,128)(2,1)}), bf16[4096,576]{0,1:T(8,128)(2,1)}) %all-gather.2.cloned.1.call-update) | async-done | bytes 4718608 | tf_op jit(solution)/shard_map/all_gather | solution.py:18
  91.3 8.0 %fusion = (f32[96,8]{1,0:T(8,128)S(1)}, f32[96,8,4096]{2,1,0:T(8,128)S(1)}) fusion(pred[96,4096]{1,0:T(8,128)(4,1)S(1)} %iota_compare_fusion, bf16[4096,576]{0,1:T(8,128)(2,1)} %all-gather.2.cloned.1.call-done, bf16[96,8,576]{2,0,1:T(8,128)(2,1)S(1)} %pad_maximum_fusion), kind=kOutput, calls=%fused_computation.2 | convolution fusion | flops 3633315072 | bytes 18582528 | tf_op jit(solution)/shard_map/rhc,ec->rhe/dot_general | solution.py:22
  99.3 3.9 %fusion.1 = f32[96,8]{1,0:T(8,128)S(1)} fusion(f32[96,8,4096]{2,1,0:T(8,128)S(1)} %get-tuple-element.3, f32[96,8]{1,0:T(8,128)S(1)} %broadcast_maximum_fusion, pred[96,4096]{1,0:T(8,128)(4,1)S(1)} %iota_compare_fusion), kind=kLoop, calls=%fused_computation.3 | loop fusion | flops 12582144 | bytes 12982272 | tf_op jit(solution)/shard_map/reduce_sum | solution.py:29
  103.2 0.0 copy-start.1
  103.2 0.0 copy-start.2
  103.2 6.1 %divide_convert_fusion = bf16[96,8,512]{2,1,0:T(8,128)(2,1)S(1)} fusion(bf16[4096,576]{0,1:T(8,128)(2,1)} %all-gather.2.cloned.1.call-done, f32[96,8,4096]{2,1,0:T(8,128)S(1)} %get-tuple-element.3, f32[96,8]{1,0:T(8,128)S(1)} %broadcast_maximum_fusion, pred[96,4096]{1,0:T(8,128)(4,1)S(1)} %iota_compare_fusion, f32[96,8]{1,0:T(8,128)S(1)} %fusion.1), kind=kOutput, calls=%fused_computation.13 | convolution fusion | flops 3234594816 | bytes 17963008 | tf_op jit(solution)/shard_map/rhe,ec->rhc/dot_general | solution.py:30
  109.3 0.0 copy-done.1
  109.3 0.0 copy-done.2
  109.3 0.7 multiply_reduce_fusion
  110.0 45.7 %psum.7 = f32[96]{0:T(128)} all-reduce(f32[96]{0:T(128)S(1)} %get-tuple-element.4), channel_id=1, replica_groups=mesh['seq'=32,'head'=16] {'head'}, use_global_device_ids=true, to_apply=%region_3.4 | all-reduce | flops 96 | bytes 768 | tf_op jit(solution)/shard_map/psum | solution.py:44
  155.7 0.7 copy_bitcast_fusion
  (1 shorter events, 0.0 us)
Async XLA Ops:
  7.2 1.9 %copy-start = (bf16[8,128,512]{2,1,0:T(8,128)(2,1)S(1)}, bf16[8,128,512]{2,1,0:T(8,128)(2,1)}, u32[]{:S(2)}) copy-start(bf16[8,128,512]{2,1,0:T(8,128)(2,1)} %param.9) | copy-start | bytes 3145732
  7.2 84.1 %all-gather.2.cloned.1.call-start = ((), (), s32[]{:S(2)}) async-start(), calls=%async_computation | async-start | bytes 4866048 | tf_op jit(solution)/shard_map/all_gather | solution.py:18
  103.2 6.1 %copy-start.1 = (bf16[8,512,128]{2,1,0:T(8,128)(2,1)S(1)}, bf16[8,512,128]{2,1,0:T(8,128)(2,1)}, u32[]{:S(2)}) copy-start(bf16[8,512,128]{2,1,0:T(8,128)(2,1)} %param.10) | copy-start | bytes 3145732
  103.2 6.1 %copy-start.2 = (f32[1024]{0:T(1024)S(1)}, f32[1024]{0:T(1024)}, u32[]{:S(2)}) copy-start(f32[1024]{0:T(1024)} %param.11) | copy-start | bytes 12292
Sparse Core Ops, SparseCore 0:
  10.1 81.1 all-gather.1
where the time goes:
time: 163 us
  waiting for transfers between devices  80.5 us (49%)
  blocking collectives  45.7 us (28%)
  matrix products  16 us (10%)
  between operations  14.1 us (9%)
  other arithmetic  4.93 us (3%)
  local copies, waits for them, and re-layouts  1.87 us (1%)
    all_gather x1, waiting for transfers between devices, on_device(): piece = lax.all_gather(kv_cache, 'seq', axis=0, tiled=True)  79.9 us
    psum x1, blocking collectives, on_device(): value = lax.psum(partial_score, 'head')  45.7 us
    dot_general x1, matrix products, on_device(): jnp.einsum('rhc,ec->rhe', q_all, piece, preferred_element_type=jnp.float32)  7.95 us
    dot_general x1, matrix products, on_device(): jnp.einsum('rhe,ec->rhc', weight.astype(jnp.bfloat16), piece[:, :latent],...  6.09 us
    reduce_sum x1, other arithmetic, on_device(): total = jnp.sum(weight, axis=2)  3.89 us
  transfers between devices with their start and end apart: 1, of which 1 were waited for; matrix products, arithmetic and copies ran while one was open for 2% of the time, Pallas kernels for 0%

commit v1 on v0

--- a/solution.py
+++ b/solution.py
@@ -15,7 +15,9 @@
         jnp.bfloat16
     )
     q_all = jnp.concatenate([q_lat, q_rope.reshape(rows, heads, -1)], axis=2)
-    piece = lax.all_gather(kv_cache, "seq", axis=0, tiled=True)
+    piece = jnp.concatenate(
+        lax.all_to_all(jnp.stack([kv_cache] * lax.axis_size("seq")), "seq", 0, 0), axis=0
+    )
     running = jnp.full((rows, heads), -1e30, jnp.float32)
     count = piece.shape[0]
     score = (

time: 163 us -> 212 us (1.30)
  the two profiles are of different devices: /device:TPU:16 before, /device:TPU:24 now
where the time goes in v1:
time: 212 us
  waiting for transfers between devices  106 us (50%)
  blocking collectives  49.1 us (23%)
  local copies, waits for them, and re-layouts  26.1 us (12%)
  matrix products  15.1 us (7%)
  starting transfers between devices  10.2 us (5%)
  other arithmetic  4.42 us (2%)
    all_to_all x1, waiting for transfers between devices, on_device(): lax.all_to_all(jnp.stack([kv_cache] * lax.axis_size('seq')), 'seq', 0, 0)  106 us
    psum x1, blocking collectives, on_device(): value = lax.psum(partial_score, 'head')  49.1 us
    reshape x2, local copies, waits for them, and re-layouts, on_device(): jnp.concatenate(lax.all_to_all(jnp.stack([kv_cache] * lax.axis_size('seq'...  13.4 us
    all_to_all x1, starting transfers between devices, on_device(): lax.all_to_all(jnp.stack([kv_cache] * lax.axis_size('seq')), 'seq', 0, 0)  10.2 us
    dot_general x1, matrix products, on_device(): jnp.einsum('rhc,ec->rhe', q_all, piece, preferred_element_type=jnp.float32)  7.94 us
    all_to_all x1, local copies, waits for them, and re-layouts, on_device(): lax.all_to_all(jnp.stack([kv_cache] * lax.axis_size('seq')), 'seq', 0, 0)  7.54 us
    dot_general x1, matrix products, on_device(): jnp.einsum('rhe,ec->rhc', weight.astype(jnp.bfloat16), piece[:, :latent],...  6.09 us
  transfers between devices with their start and end apart: 1, of which 1 were waited for; matrix products, arithmetic and copies ran while one was open for 0% of the time, Pallas kernels for 0%

profile of v1, /device:TPU:24, one launch (start us, length us, event | category | flops | bytes accessed | tf_op | source)
XLA Modules:
  0.0 212.0 jit_solution(3584351704391941209)
XLA Ops:
  0.6 0.0 copy-start
  0.6 4.2 %stack.2 = bf16[32,128,576]{1,2,0:T(8,128)(2,1)} broadcast(bf16[128,576]{0,1:T(8,128)(2,1)} %param.12), dimensions={1,2} | broadcast | bytes 4866048 | tf_op jit(solution)/shard_map/stack | solution.py:19
  4.9 0.0 copy-start.2
  4.9 0.0 copy-start.1
  4.9 0.0 copy-start.3
  4.9 10.2 %all-to-all-start = ((bf16[32,128,576]{1,2,0:T(8,128)(2,1)}), bf16[32,128,576]{1,2,0:T(8,128)(2,1)}, u32[]{:S(2)}, u32[]{:S(2)}) async-start(bf16[32,128,576]{1,2,0:T(8,128)(2,1)} %stack.2), calls=%async_computation | async-start | bytes 9437184 | tf_op jit(solution)/shard_map/all_to_all | solution.py:19
  15.1 0.0 copy-done.2
  15.1 0.1 copy.13
  15.2 0.2 copy.14
  15.4 0.0 copy-done
  15.4 0.0 copy-done.1
  15.4 0.4 fusion.9
  15.8 0.1 pad_maximum_fusion
  15.9 0.0 copy-done.3
  15.9 0.3 iota_compare_fusion
  16.2 106.3 %all-to-all-done = bf16[32,128,576]{1,2,0:T(8,128)(2,1)} async-done(((bf16[32,128,576]{1,2,0:T(8,128)(2,1)}), bf16[32,128,576]{1,2,0:T(8,128)(2,1)}, u32[]{:S(2)}, u32[]{:S(2)}) %all-to-all-start) | async-done | bytes 4718624 | tf_op jit(solution)/shard_map/all_to_all | solution.py:19
  122.4 7.5 %copy.15 = bf16[32,128,576]{1,0,2:T(8,128)(2,1)} copy(bf16[32,128,576]{1,2,0:T(8,128)(2,1)} %all-to-all-done) | data formatting | bytes 9437184 | tf_op jit(solution)/shard_map/all_to_all | solution.py:19
  130.0 8.2 %reshape.53 = bf16[4096,576,1]{0,1,2:T(8,128)(2,1)} reshape(bf16[32,128,576]{1,0,2:T(8,128)(2,1)} %copy.15) | data formatting | bytes 9437184 | tf_op jit(solution)/shard_map/reshape | solution.py:18
  138.1 7.9 %fusion = (f32[96,8]{1,0:T(8,128)S(1)}, f32[96,8,4096]{2,1,0:T(8,128)S(1)}) fusion(pred[96,4096]{1,0:T(8,128)(4,1)S(1)} %iota_compare_fusion, bf16[4096,576,1]{0,1,2:T(8,128)(2,1)} %reshape.53, bf16[96,8,576]{2,0,1:T(8,128)(2,1)S(1)} %pad_maximum_fusion), kind=kOutput, calls=%fused_computation.2 | convolution fusion | flops 3633315072 | bytes 18582528 | tf_op jit(solution)/shard_map/rhc,ec->rhe/dot_general | solution.py:24
  146.1 4.0 %fusion.1 = f32[96,8]{1,0:T(8,128)S(1)} fusion(f32[96,8,4096]{2,1,0:T(8,128)S(1)} %get-tuple-element.3, f32[96,8]{1,0:T(8,128)S(1)} %broadcast_maximum_fusion, pred[96,4096]{1,0:T(8,128)(4,1)S(1)} %iota_compare_fusion), kind=kLoop, calls=%fused_computation.3 | loop fusion | flops 12582144 | bytes 12982272 | tf_op jit(solution)/shard_map/reduce_sum | solution.py:31
  150.1 5.2 %copy_bitcast_fusion = bf16[4096,576]{0,1:T(8,128)(2,1)} fusion(bf16[32,128,576]{1,2,0:T(8,128)(2,1)} %all-to-all-done), kind=kLoop, calls=%fused_computation.10 | loop fusion | bytes 9437184 | tf_op jit(solution)/shard_map/reshape | solution.py:18
  155.3 0.0 copy-start.4
  155.4 0.0 copy-start.5
  155.4 6.1 %divide_convert_fusion = bf16[96,8,512]{2,1,0:T(8,128)(2,1)S(1)} fusion(bf16[4096,576]{0,1:T(8,128)(2,1)} %copy_bitcast_fusion, f32[96,8,4096]{2,1,0:T(8,128)S(1)} %get-tuple-element.3, f32[96,8]{1,0:T(8,128)S(1)} %broadcast_maximum_fusion, pred[96,4096]{1,0:T(8,128)(4,1)S(1)} %iota_compare_fusion, f32[96,8]{1,0:T(8,128)S(1)} %fusion.1), kind=kOutput, calls=%fused_computation.12 | convolution fusion | flops 3234594816 | bytes 17963008 | tf_op jit(solution)/shard_map/rhe,ec->rhc/dot_general | solution.py:32
  161.5 0.0 copy-done.4
  161.5 0.0 copy-done.5
  161.5 0.7 multiply_reduce_fusion
  162.2 49.1 %psum.7 = f32[96]{0:T(128)} all-reduce(f32[96]{0:T(128)S(1)} %get-tuple-element.4), channel_id=1, replica_groups=mesh['seq'=32,'head'=16] {'head'}, use_global_device_ids=true, to_apply=%region_3.4 | all-reduce | flops 96 | bytes 768 | tf_op jit(solution)/shard_map/psum | solution.py:46
  211.3 0.7 copy_bitcast_fusion.1
  (1 shorter events, 0.0 us)
Async XLA Ops:
  0.6 14.8 %copy-start = (bf16[8,128,512]{2,1,0:T(8,128)(2,1)S(1)}, bf16[8,128,512]{2,1,0:T(8,128)(2,1)}, u32[]{:S(2)}) copy-start(bf16[8,128,512]{2,1,0:T(8,128)(2,1)} %param.9) | copy-start | bytes 3145732
  4.9 10.2 %copy-start.2 = (bf16[96,512]{1,0:T(8,128)(2,1)S(1)}, bf16[96,512]{1,0:T(8,128)(2,1)}, u32[]{:S(2)}) copy-start(bf16[96,512]{1,0:T(8,128)(2,1)} %param.8) | copy-start | bytes 294916
  4.9 10.5 %copy-start.1 = (bf16[96,1024]{1,0:T(8,128)(2,1)S(1)}, bf16[96,1024]{1,0:T(8,128)(2,1)}, u32[]{:S(2)}) copy-start(bf16[96,1024]{1,0:T(8,128)(2,1)} %param.7) | copy-start | bytes 589828
  4.9 11.0 %copy-start.3 = (s32[96]{0:T(128)S(1)}, s32[96]{0:T(128)}, u32[]{:S(2)}) copy-start(s32[96]{0:T(128)} %param.13) | copy-start | bytes 1156
  4.9 117.6 %all-to-all-start = ((bf16[32,128,576]{1,2,0:T(8,128)(2,1)}), bf16[32,128,576]{1,2,0:T(8,128)(2,1)}, u32[]{:S(2)}, u32[]{:S(2)}) async-start(bf16[32,128,576]{1,2,0:T(8,128)(2,1)} %stack.2), calls=%async_computation | async-start | bytes 9437184 | tf_op jit(solution)/shard_map/all_to_all | solution.py:19
  155.3 6.1 %copy-start.4 = (bf16[8,512,128]{2,1,0:T(8,128)(2,1)S(1)}, bf16[8,512,128]{2,1,0:T(8,128)(2,1)}, u32[]{:S(2)}) copy-start(bf16[8,512,128]{2,1,0:T(8,128)(2,1)} %param.10) | copy-start | bytes 3145732
  155.4 6.1 %copy-start.5 = (f32[1024]{0:T(1024)S(1)}, f32[1024]{0:T(1024)}, u32[]{:S(2)}) copy-start(f32[1024]{0:T(1024)} %param.11) | copy-start | bytes 12292
